TPU v7x, 32 devices: a whole 2x2x4 slice. The times are simulated.
32 devices in a mesh: ch: 4 (over z), ha: 2 (over x), dp: 4 (over y, core).
Axes of the slice: x: 2, y: 2, z: 4, core: 2. Of those that a mesh axis runs over, the one named last changes fastest.
Arguments:
- features: bfloat16 [384, 4, 4, 4, 128], P('ch', 'dp', None, 'ha'), may hold values from -26 to 26
- frame_count: int32 [4], P('dp'), may hold values from 1 to 4, as said below
- norm1_gain: float32 [384], P('ch'), may hold values from 0.5 to 2
- norm1_shift: float32 [384], P('ch'), may hold values from -3 to 3
- qkv_weight: bfloat16 [384, 1152], replicated, may hold values from -0.51031036 to 0.51031036
- qkv_bias: float32 [1152], replicated, may hold values from -3 to 3
- out_weight: bfloat16 [384, 384], replicated, may hold values from -0.3125 to 0.3125
- out_bias: float32 [384], replicated, may hold values from -3 to 3
- norm2_gain: float32 [384], P('ch'), may hold values from 0.5 to 2
- norm2_shift: float32 [384], P('ch'), may hold values from -3 to 3
- conv_weight: bfloat16 [3, 3, 3, 384, 384], P(None, None, None, 'ch'), may hold values from -0.0625 to 0.0625
- conv_bias: float32 [384], P('ch'), may hold values from -3 to 3
- cotangent: bfloat16 [384, 4, 4, 4, 128], P('ch', 'dp', None, 'ha'), may hold values from -0.0625 to 0.0625
Outputs:
- mixed: bfloat16 [384, 4, 4, 4, 128], P('ch', 'dp', None, 'ha')
- weight_grad: float32 [3, 3, 3, 384, 384], P(None, None, None, 'ch')
Inputs may be any that keep to these rules, and one draw needn't show every extreme that they name: `frame_count`: some clip has all 4 frames valid and some clip only one.
All inputs are finite; a program needn't handle non-finite values.
Results may differ from a plain program's by a relative error of at most 0.015.
Values may be sent and summed in bfloat16 or wider, within the bound.
A program may use at most 64 MiB of HBM per device.

v0:
```python
import jax
import jax.numpy as jnp
from jax import lax
from jax.sharding import PartitionSpec as P

GROUPS = 32
EPS = 1e-06


def padded_2(x, sides, width):
    for axis, dim in sides:
        count, length = (lax.axis_size(axis), x.shape[dim])
        up = [(i, (i + 1) % count) for i in range(count - 1)]
        down = [(j, i) for i, j in up]
        last = lax.slice_in_dim(x, length - width, length, axis=dim)
        leading = lax.slice_in_dim(x, 0, width, axis=dim)
        before = lax.ppermute(last, axis, up)
        after = lax.ppermute(leading, axis, down)
        x = jnp.concatenate([before, x, after], axis=dim)
    return x


def frame_mask(frame_count, frames):
    position = lax.broadcasted_iota(jnp.int32, (frame_count.shape[0], frames), 1)
    return (position < frame_count[:, None]).astype(jnp.float32)


def moments(values, mask, groups):
    chans, clips, frames, rows, cols = values.shape
    data = values.astype(jnp.float32).reshape(groups, chans // groups, clips, frames, rows * cols)
    first = jnp.einsum("gkbfp,bf->gb", data, mask)
    second = jnp.einsum("gkbfp,bf->gb", data * data, mask)
    return (first, second)


def normalize(values, first, second, count, gain, shift, groups):
    chans, clips, frames, rows, cols = values.shape
    mean = first / count[None, :]
    var = second / count[None, :] - mean * mean
    scale = lax.rsqrt(var + EPS)
    data = values.astype(jnp.float32).reshape(groups, chans // groups, clips, frames, rows * cols)
    normed = (data - mean[:, None, :, None, None]) * scale[:, None, :, None, None]
    normed = normed.reshape(values.shape)
    return normed * gain[:, None, None, None, None] + shift[:, None, None, None, None]


def attend(carry, queries, keys, values, scale):
    top, total, acc = carry
    scores = jnp.einsum("itc,isc->its", queries, keys, preferred_element_type=jnp.float32) * scale
    new_top = jnp.max(scores, axis=2)
    factor = jnp.exp(top - new_top)
    weights = jnp.exp(scores - new_top[..., None])
    total = total * factor + jnp.sum(weights, axis=2)
    acc = acc * factor[..., None] + jnp.einsum(
        "its,isc->itc", weights.astype(jnp.bfloat16), values, preferred_element_type=jnp.float32
    )
    return (new_top, total, acc)


def tap_stack(padded, time_tap, frames, rows, cols):
    windows = []
    for row_tap in range(3):
        for col_tap in range(3):
            windows.append(
                padded[
                    :,
                    :,
                    time_tap : time_tap + frames,
                    row_tap : row_tap + rows,
                    col_tap : col_tap + cols,
                ]
            )
    return jnp.concatenate(windows, axis=0)


def body(
    features,
    frame_count,
    norm1_gain,
    norm1_shift,
    qkv_weight,
    qkv_bias,
    out_weight,
    out_bias,
    norm2_gain,
    norm2_shift,
    conv_weight,
    conv_bias,
    cotangent,
):
    chans, clips, frames, rows, cols = features.shape
    groups = GROUPS // lax.axis_size("ch")
    mask = frame_mask(frame_count, frames)
    count = frame_count.astype(jnp.float32) * (chans // groups * rows * lax.axis_size("ha") * cols)
    first, second = moments(features, mask, groups)
    first, second = lax.psum((first, second), "ha")
    normed = normalize(features, first, second, count, norm1_gain, norm1_shift, groups).astype(
        jnp.bfloat16
    )
    by_frame = lax.all_to_all(normed, "ch", split_axis=2, concat_axis=0, tiled=True)
    width = by_frame.shape[0]
    items = clips * by_frame.shape[2]
    tok_rows = rows * cols
    tokens = by_frame.reshape(width, items, tok_rows)
    queries = lax.dot_general(
        tokens, qkv_weight[:, :width], (((0,), (0,)), ((), ())), preferred_element_type=jnp.float32
    )
    queries = (queries + qkv_bias[:width]).astype(jnp.bfloat16)
    scale = width ** (-0.5)
    start_carry = (
        jnp.full((items, tok_rows), -jnp.inf, jnp.float32),
        jnp.zeros((items, tok_rows), jnp.float32),
        jnp.zeros((items, tok_rows, width), jnp.float32),
    )
    pairs = lax.dot_general(
        tokens, qkv_weight[:, width:], (((0,), (0,)), ((), ())), preferred_element_type=jnp.float32
    )
    pairs = (pairs + qkv_bias[width:]).astype(jnp.bfloat16)
    piece = lax.all_gather(pairs, "ha", axis=1, tiled=True)
    top, total, acc = attend(start_carry, queries, piece[..., :width], piece[..., width:], scale)
    attended = (acc / total[..., None]).astype(jnp.bfloat16)
    projected = lax.dot_general(
        out_weight, attended, (((0,), (2,)), ((), ())), preferred_element_type=jnp.float32
    )
    projected = (projected + out_bias[:, None, None]).astype(jnp.bfloat16).reshape(by_frame.shape)
    update = lax.all_to_all(projected, "ch", split_axis=0, concat_axis=2, tiled=True)
    hidden = (features.astype(jnp.float32) + update.astype(jnp.float32)).astype(jnp.bfloat16)
    first, second = moments(hidden, mask, groups)
    first, second = lax.psum((first, second), "ha")
    gated = jax.nn.silu(
        normalize(hidden, first, second, count, norm2_gain, norm2_shift, groups)
    ).astype(jnp.bfloat16)
    with_rows = padded_2(gated, (("ha", 3),), 1)
    padded = jnp.pad(with_rows, ((0, 0), (0, 0), (2, 0), (0, 0), (1, 1)))
    stacks = [tap_stack(padded, time_tap, frames, rows, cols) for time_tap in range(3)]
    amount = chans * lax.axis_size("ch")
    summed = jnp.zeros((amount, clips, frames, rows, cols), jnp.float32)
    for time_tap in range(3):
        part = conv_weight[time_tap].reshape(9 * chans, amount)
        summed = summed + lax.dot_general(
            part, stacks[time_tap], (((0,), (0,)), ((), ())), preferred_element_type=jnp.float32
        )
    conv_out = lax.psum_scatter(
        summed.astype(jnp.bfloat16), "ch", scatter_dimension=0, tiled=True
    ).astype(jnp.float32)
    mixed = mask[None, :, :, None, None] * (
        hidden.astype(jnp.float32) + conv_out + conv_bias[:, None, None, None, None]
    )
    mixed = mixed.astype(jnp.bfloat16)
    masked_cot = cotangent * mask.astype(jnp.bfloat16)[None, :, :, None, None]
    full_width = chans * lax.axis_size("ch")
    carry = jnp.zeros((3, 9 * chans, full_width), jnp.float32)
    piece = lax.all_gather(masked_cot, "ch", axis=0, tiled=True)
    start = jnp.int32(0)
    for time_tap in range(3):
        part = lax.dot_general(
            stacks[time_tap],
            piece,
            (((1, 2, 3, 4), (1, 2, 3, 4)), ((), ())),
            preferred_element_type=jnp.float32,
        )
        carry = lax.dynamic_update_slice(
            carry, part[None], (jnp.int32(time_tap), jnp.int32(0), start)
        )
    grad_table = carry
    grad_table = grad_table.reshape(3, 3, 3, chans, full_width)
    weight_grad = lax.psum(grad_table.astype(jnp.bfloat16), ("ha", "dp")).astype(jnp.float32)
    return (mixed, weight_grad)


def solution(mesh):
    placed = (
        P("ch", "dp", None, "ha", None),
        P("dp"),
        P("ch"),
        P("ch"),
        P(),
        P(),
        P(),
        P(),
        P("ch"),
        P("ch"),
        P(None, None, None, "ch", None),
        P("ch"),
        P("ch", "dp", None, "ha", None),
    )
    return jax.shard_map(
        body,
        mesh=mesh,
        in_specs=placed,
        out_specs=(P("ch", "dp", None, "ha", None), P(None, None, None, "ch", None)),
        check_vma=False,
    )
```

profile of v0, /device:TPU:0, one launch (start us, length us, event | category | flops | bytes accessed | tf_op | source)
XLA Modules:
  0.0 170.4 jit_solution(4983406673391585404)
XLA Ops:
  8.7 1.1 fusion.57
  10.4 5.9 %all-reduce.3 = (f32[8,1]{0,1:T(1,128)S(1)}, f32[8,1]{0,1:T(1,128)S(1)}) all-reduce(f32[8,1]{0,1:T(1,128)S(1)} %convolution_bitcast_fusion.3, f32[8,1]{0,1:T(1,128)S(1)} %convolution_bitcast_fusion.2), channel_id=1, replica_groups=mesh['ch'=4,'ha'=2,'dp'=4] {'ha'}, use_global_device_ids=true, to_apply=%region_2.0 | all-reduce | flops 16 | bytes 128 | tf_op jit(solution)/shard_map/psum | solution.py:96
  16.6 1.8 %fusion.78 = bf16[96,1,4,2,128]{4,0,3,1,2:T(8,128)(2,1)} fusion(f32[96]{0:T(128)} %param.16, f32[96]{0:T(128)} %param.15, f32[96]{0:T(128)S(1)} %mul.117, f32[96]{0:T(128)S(1)} %sub.66, bf16[96,1,4,2,128]{4,3,2,1,0:T(2,128)(2,1)} %param.13), kind=kLoop, calls=%fused_computation.84 | loop fusion | flops 589824 | bytes 394752 | tf_op jit(solution)/shard_map/convert_element_type | solution.py:97
  18.4 5.5 %all-to-all-start = ((bf16[96,1,4,2,128]{4,0,3,1,2:T(8,128)(2,1)}), bf16[96,1,4,2,128]{4,0,3,1,2:T(8,128)(2,1)S(1)}, u32[]{:S(2)}, u32[]{:S(2)}) async-start(bf16[96,1,4,2,128]{4,0,3,1,2:T(8,128)(2,1)} %fusion.78), calls=%async_computation | async-start | bytes 393216 | tf_op jit(solution)/shard_map/all_to_all | solution.py:100
  24.0 0.7 slice.120
  24.7 5.5 %all-to-all-done = bf16[96,1,4,2,128]{4,0,3,1,2:T(8,128)(2,1)S(1)} async-done(((bf16[96,1,4,2,128]{4,0,3,1,2:T(8,128)(2,1)}), bf16[96,1,4,2,128]{4,0,3,1,2:T(8,128)(2,1)S(1)}, u32[]{:S(2)}, u32[]{:S(2)}) %all-to-all-start) | async-done | bytes 196640 | tf_op jit(solution)/shard_map/all_to_all | solution.py:100
  30.2 0.2 copy.32
  30.4 1.5 fusion.37
  31.8 8.9 %all-gather = bf16[512,768]{1,0:T(8,128)(2,1)S(1)} all-gather(bf16[256,768]{1,0:T(8,128)(2,1)S(1)} %fusion.37), channel_id=2, replica_groups=mesh['ch'=4,'ha'=2,'dp'=4] {'ha'}, dimensions={0}, use_global_device_ids=true | all-gather | bytes 1179648 | tf_op jit(solution)/shard_map/all_gather | solution.py:119
  40.8 1.6 fusion.104
  42.4 0.2 fusion.51
  42.7 0.6 fusion.46
  43.3 0.9 copy.33
  44.1 3.5 %all-to-all-start.1 = ((bf16[384,1,1,2,128]{4,3,2,1,0:T(2,128)(2,1)}), bf16[384,1,1,2,128]{4,3,2,1,0:T(2,128)(2,1)S(1)}, u32[]{:S(2)}, u32[]{:S(2)}) async-start(bf16[384,1,1,2,128]{4,3,2,1,0:T(2,128)(2,1)} %copy.33), calls=%async_computation.1 | async-start | bytes 393216 | tf_op jit(solution)/shard_map/all_to_all | solution.py:126
  47.8 6.1 %all-to-all-done.1 = bf16[384,1,1,2,128]{4,3,2,1,0:T(2,128)(2,1)S(1)} async-done(((bf16[384,1,1,2,128]{4,3,2,1,0:T(2,128)(2,1)}), bf16[384,1,1,2,128]{4,3,2,1,0:T(2,128)(2,1)S(1)}, u32[]{:S(2)}, u32[]{:S(2)}) %all-to-all-start.1) | async-done | bytes 196640 | tf_op jit(solution)/shard_map/all_to_all | solution.py:126
  54.0 0.2 fusion.68
  54.8 17.3 %all_gather.7 = bf16[384,1,4,2,128]{4,0,3,2,1:T(8,128)(2,1)} all-gather(bf16[96,1,4,2,128]{4,0,3,2,1:T(8,128)(2,1)S(1)} %copy_multiply_fusion), channel_id=1, replica_groups=mesh['ch'=4,'ha'=2,'dp'=4] {'ch'}, dimensions={0}, use_global_device_ids=true | all-gather | bytes 983040 | tf_op jit(solution)/shard_map/all_gather | solution.py:153
  72.1 4.9 %all-reduce.2 = (f32[8,1]{0,1:T(1,128)S(1)}, f32[8,1]{0,1:T(1,128)S(1)}) all-reduce(f32[8,1]{0,1:T(1,128)S(1)} %convolution_bitcast_fusion.1, f32[8,1]{0,1:T(1,128)S(1)} %convolution_bitcast_fusion), channel_id=1, replica_groups=mesh['ch'=4,'ha'=2,'dp'=4] {'ha'}, use_global_device_ids=true, to_apply=%region_10.11 | all-reduce | flops 16 | bytes 128 | tf_op jit(solution)/shard_map/psum | solution.py:129
  77.3 0.3 fusion.67
  77.7 3.4 %collective-permute-start = (bf16[96,1,4,1,128]{4,0,3,2,1:T(8,128)(2,1)S(1)}, bf16[96,1,4,1,128]{4,0,3,2,1:T(8,128)(2,1)S(1)}, u32[]{:S(2)}, u32[]{:S(2)}) collective-permute-start(bf16[96,1,4,1,128]{4,0,3,2,1:T(8,128)(2,1)S(1)} %get-tuple-element.47), channel_id=1, source_target_pairs={{0,4},{1,5},{2,6},{3,7},{8,12},{9,13},{10,14},{11,15},{16,20},{17,... | collective-permute-start | bytes 294920 | tf_op jit(solution)/shard_map/ppermute | solution.py:17
  81.1 1.3 collective-permute-start.1
  82.4 1.3 fusion.102
  83.7 3.9 %collective-permute-done.1 = bf16[96,1,4,1,128]{4,0,3,2,1:T(8,128)(2,1)S(1)} collective-permute-done((bf16[96,1,4,1,128]{4,0,3,2,1:T(8,128)(2,1)S(1)}, bf16[96,1,4,1,128]{4,0,3,2,1:T(8,128)(2,1)S(1)}, u32[]{:S(2)}, u32[]{:S(2)}) %collective-permute-start.1) | collective-permute-done | bytes 98336 | tf_op jit(solution)/shard_map/ppermute | solution.py:18
  87.6 0.4 fusion.41
  88.1 0.2 slice_dynamic-update-slice_fusion.13
  88.3 0.2 slice_dynamic-update-slice_fusion.12
  88.6 0.2 slice_dynamic-update-slice_fusion.10
  88.9 0.3 slice_dynamic-update-slice_fusion.9
  89.2 0.1 slice_dynamic-update-slice_fusion.8
  89.4 0.4 constant_dynamic-update-slice_fusion
  89.8 0.3 slice_dynamic-update-slice_fusion.7
  90.1 0.3 slice_dynamic-update-slice_fusion.6
  90.4 1.1 fusion.19
  91.6 0.2 dynamic_update_slice.9
  91.8 0.1 slice_dynamic-update-slice_fusion
  91.9 0.2 copy-done.9
  92.1 1.2 fusion.25
  93.3 1.2 fusion.31
  94.5 1.3 copy-done.1
  95.8 0.2 reduce-scatter.2.cloned.1.call-start
  96.1 2.8 %fusion.11 = f32[4,2,128,384]{2,3,1,0:T(8,128)S(1)} fusion(bf16[864,384,1,1]{1,0,3,2:T(8,128)(2,1)} %bitcast.175, bf16[864,1,4,2,128]{4,0,3,2,1:T(8,128)(2,1)} %copy-done.9), kind=kOutput, calls=%fused_computation.14 | convolution fusion | flops 679477248 | bytes 4005888 | tf_op jit(solution)/shard_map/dot_general | solution.py:140
  98.9 1.0 fusion.15
  100.0 0.4 copy-done.3
  100.4 2.0 %fusion.34 = bf16[384,1,4,2,128]{4,0,3,2,1:T(8,128)(2,1)} fusion(bf16[864,384,1,1]{1,0,3,2:T(8,128)(2,1)S(1)} %bitcast.169, bf16[864,1,4,2,128]{4,0,3,2,1:T(8,128)(2,1)S(1)} %copy-done.3, f32[4,2,128,384]{2,3,1,0:T(8,128)S(1)} %fusion.15, f32[4,2,128,384]{2,3,1,0:T(8,128)S(1)} %fusion.11), kind=kOutput, calls=%fused_computation.26 | convolution fusion | flops 680656896 | bytes 6365184 | tf_op jit(solution)/shard_map/dot_general | solution.py:140
  102.4 54.7 %all-reduce.6.cloned.1.call-done = bf16[3,3,3,96,384]{4,3,2,1,0:T(8,128)(2,1)} async-done(((bf16[3,3,3,96,384]{4,3,2,1,0:T(8,128)(2,1)}), bf16[3,3,3,96,384]{4,3,2,1,0:T(8,128)(2,1)}) %all-reduce.6.cloned.1.call-update) | async-done | bytes 1990672 | tf_op jit(solution)/shard_map/psum | solution.py:167
  157.1 4.0 %convert_element_type.145 = f32[3,3,3,96,384]{4,3,2,1,0:T(8,128)} convert(bf16[3,3,3,96,384]{4,3,2,1,0:T(8,128)(2,1)} %all-reduce.6.cloned.1.call-done) | non-fusion elementwise | flops 995328 | bytes 5971968 | tf_op jit(solution)/shard_map/convert_element_type | solution.py:167
  161.1 1.1 fusion.71
  162.1 0.8 copy.40
  (68 shorter events, 2.4 us)
Async XLA Ops:
  8.0 34.6 %copy-start = (bf16[384,384]{1,0:T(8,128)(2,1)S(1)}, bf16[384,384]{1,0:T(8,128)(2,1)}, u32[]{:S(2)}) copy-start(bf16[384,384]{1,0:T(8,128)(2,1)} %param.19) | copy-start | bytes 884740
  18.4 22.4 %slice-start = ((f32[1152]{0:T(1024)}), f32[384]{0:T(512)S(1)}, s32[]{:S(2)}) async-start(f32[1152]{0:T(1024)} %param.18), calls=%async_computation.5 | async-start | bytes 4096 | tf_op jit(solution)/shard_map/slice | solution.py:108
  18.4 11.8 %all-to-all-start = ((bf16[96,1,4,2,128]{4,0,3,1,2:T(8,128)(2,1)}), bf16[96,1,4,2,128]{4,0,3,1,2:T(8,128)(2,1)S(1)}, u32[]{:S(2)}, u32[]{:S(2)}) async-start(bf16[96,1,4,2,128]{4,0,3,1,2:T(8,128)(2,1)} %fusion.78), calls=%async_computation | async-start | bytes 393216 | tf_op jit(solution)/shard_map/all_to_all | solution.py:100
  31.8 10.8 %copy-start.15 = (f32[384]{0:T(512)S(1)}, f32[384]{0:T(512)}, u32[]{:S(2)}) copy-start(f32[384]{0:T(512)} %param.20) | copy-start | bytes 4612
  42.6 5.1 %copy-start.8 = (bf16[96,1,4,2,128]{4,3,2,1,0:T(2,128)(2,1)S(1)}, bf16[96,1,4,2,128]{4,3,2,1,0:T(2,128)(2,1)}, u32[]{:S(2)}) copy-start(bf16[96,1,4,2,128]{4,3,2,1,0:T(2,128)(2,1)} %param.25) | copy-start | bytes 589828
  42.6 11.3 %copy-start.5 = (bf16[96,1,4,2,128]{4,3,2,1,0:T(2,128)(2,1)S(1)}, bf16[96,1,4,2,128]{4,3,2,1,0:T(2,128)(2,1)}, u32[]{:S(2)}) copy-start(bf16[96,1,4,2,128]{4,3,2,1,0:T(2,128)(2,1)} %param.13) | copy-start | bytes 589828
  43.2 34.1 %copy-start.12 = (f32[96]{0:T(128)S(1)}, f32[96]{0:T(128)}, u32[]{:S(2)}) copy-start(f32[96]{0:T(128)} %param.22) | copy-start | bytes 1156
  43.3 34.1 %copy-start.13 = (f32[96]{0:T(128)S(1)}, f32[96]{0:T(128)}, u32[]{:S(2)}) copy-start(f32[96]{0:T(128)} %param.21) | copy-start | bytes 1156
  44.1 38.3 %copy-start.4 = (bf16[3,3,3,96,384]{4,3,2,1,0:T(8,128)(2,1)S(1)}, bf16[3,3,3,96,384]{4,3,2,1,0:T(8,128)(2,1)}, u32[]{:S(2)}) copy-start(bf16[3,3,3,96,384]{4,3,2,1,0:T(8,128)(2,1)} %param.23) | copy-start | bytes 5971972
  44.1 9.8 %all-to-all-start.1 = ((bf16[384,1,1,2,128]{4,3,2,1,0:T(2,128)(2,1)}), bf16[384,1,1,2,128]{4,3,2,1,0:T(2,128)(2,1)S(1)}, u32[]{:S(2)}, u32[]{:S(2)}) async-start(bf16[384,1,1,2,128]{4,3,2,1,0:T(2,128)(2,1)} %copy.33), calls=%async_computation.1 | async-start | bytes 393216 | tf_op jit(solution)/shard_map/all_to_all | solution.py:126
  47.6 109.4 %all-reduce.6.cloned.1.call-start = ((), (), s32[]{:S(2)}) async-start(), calls=%async_computation.4 | async-start | bytes 3981312 | tf_op jit(solution)/shard_map/psum | solution.py:167
  77.7 6.1 %collective-permute-start = (bf16[96,1,4,1,128]{4,0,3,2,1:T(8,128)(2,1)S(1)}, bf16[96,1,4,1,128]{4,0,3,2,1:T(8,128)(2,1)S(1)}, u32[]{:S(2)}, u32[]{:S(2)}) collective-permute-start(bf16[96,1,4,1,128]{4,0,3,2,1:T(8,128)(2,1)S(1)} %get-tuple-element.47), channel_id=1, source_target_pairs={{0,4},{1,5},{2,6},{3,7},{8,12},{9,13},{10,14},{11,15},{16,20},{17,... | collective-permute-start | bytes 294920 | tf_op jit(solution)/shard_map/ppermute | solution.py:17
  81.1 6.5 %collective-permute-start.1 = (bf16[96,1,4,1,128]{4,0,3,2,1:T(8,128)(2,1)S(1)}, bf16[96,1,4,1,128]{4,0,3,2,1:T(8,128)(2,1)S(1)}, u32[]{:S(2)}, u32[]{:S(2)}) collective-permute-start(bf16[96,1,4,1,128]{4,0,3,2,1:T(8,128)(2,1)S(1)} %get-tuple-element.48), channel_id=1, source_target_pairs={{4,0},{5,1},{6,2},{7,3},{12,8},{13,9},{14,10},{15,11},{20,16},{21,... | collective-permute-start | bytes 294920 | tf_op jit(solution)/shard_map/ppermute | solution.py:18
  89.2 1.1 copy-start.6
  90.3 1.2 copy-start.10
  90.3 1.8 %copy-start.9 = (bf16[864,1,4,2,128]{4,0,3,2,1:T(8,128)(2,1)}, bf16[864,1,4,2,128]{4,0,3,2,1:T(8,128)(2,1)S(1)}, u32[]{:S(2)}) copy-start(bf16[864,1,4,2,128]{4,0,3,2,1:T(8,128)(2,1)S(1)} %get-tuple-element.24) | copy-start | bytes 5308420
  91.9 1.4 copy-start.2
  94.5 1.3 copy-start.1
  95.8 65.2 %reduce-scatter.2.cloned.1.call-start = ((), (), s32[]{:S(2)}) async-start(), calls=%async_computation.3 | async-start | bytes 983040 | tf_op jit(solution)/shard_map/reduce_scatter | solution.py:143
  96.1 2.8 %copy-start.7 = (bf16[1,3,3,96,384]{4,3,2,1,0:T(8,128)(2,1)S(1)}, bf16[1,3,3,96,384]{4,3,2,1,0:T(8,128)(2,1)}, u32[]{:S(2)}) copy-start(bf16[1,3,3,96,384]{4,3,2,1,0:T(8,128)(2,1)} %get-tuple-element.22) | copy-start | bytes 1990660
  96.1 2.8 %copy-start.11 = (bf16[864,1,4,2,128]{4,0,3,2,1:T(8,128)(2,1)S(1)}, bf16[864,1,4,2,128]{4,0,3,2,1:T(8,128)(2,1)}, u32[]{:S(2)}) copy-start(bf16[864,1,4,2,128]{4,0,3,2,1:T(8,128)(2,1)} %copy-done.10) | copy-start | bytes 5308420
  98.9 1.5 copy-start.3
  102.4 58.7 %copy-start.14 = (f32[96]{0:T(128)S(1)}, f32[96]{0:T(128)}, u32[]{:S(2)}) copy-start(f32[96]{0:T(128)} %param.24) | copy-start | bytes 1156
Sparse Core Ops, SparseCore 0:
  96.0 61.0 all-reduce.5
Sparse Core Ops, SparseCore 1:
  102.5 22.9 reduce-scatter.1
where the time goes:
time: 171 us; the launch traced here: 170 us
  waiting for transfers between devices  70.3 us (41%)
  blocking collectives  37 us (22%)
  between operations  16.6 us (10%)
  starting transfers between devices  14 us (8%)
  matrix products  13.4 us (8%)
  other arithmetic  10.1 us (6%)
  local copies, waits for them, and re-layouts  9.05 us (5%)
    psum x1, waiting for transfers between devices, body(): lax.psum(grad_table.astype(jnp.bfloat16), ('ha', 'dp')).astype(jnp.float32)  54.7 us
    all_gather x1, blocking collectives, body(): piece = lax.all_gather(masked_cot, 'ch', axis=0, tiled=True)  17.3 us
    psum x2, blocking collectives, body(): first, second = lax.psum((first, second), 'ha')  10.8 us
    all_gather x1, blocking collectives, body(): piece = lax.all_gather(pairs, 'ha', axis=1, tiled=True)  8.94 us
    all_to_all x1, waiting for transfers between devices, body(): lax.all_to_all(projected, 'ch', split_axis=0, concat_axis=2, tiled=True)  6.12 us
    dot_general x3, matrix products, body(): lax.dot_general(part, stacks[time_tap], (((0,), (0,)), ((), ())), preferr...  5.78 us
    all_to_all x1, waiting for transfers between devices, body(): lax.all_to_all(normed, 'ch', split_axis=2, concat_axis=0, tiled=True)  5.55 us
    all_to_all x1, starting transfers between devices, body(): lax.all_to_all(normed, 'ch', split_axis=2, concat_axis=0, tiled=True)  5.54 us
  transfers between devices with their start and end apart: 6, of which 4 were waited for; matrix products, arithmetic and copies ran while one was open for 7% of the time, Pallas kernels for 0%

commit v1 on v0

--- a/solution.py
+++ b/solution.py
@@ -5,6 +5,19 @@
 
 GROUPS = 32
 EPS = 1e-06
+
+
+def gather_around(x, axis, dim):
+    size, index, rows = (lax.axis_size(axis), lax.axis_index(axis), x.shape[dim])
+    forward = [(i, (i + 1) % size) for i in range(size)]
+    out = jnp.zeros((*x.shape[:dim], size * rows, *x.shape[dim + 1 :]), x.dtype)
+    block = x
+    for step in range(size):
+        owner = (index - step) % size
+        out = lax.dynamic_update_slice_in_dim(out, block, owner * rows, axis=dim)
+        if step < size - 1:
+            block = lax.ppermute(block, axis, forward)
+    return out
 
 
 def padded_2(x, sides, width):
@@ -150,7 +163,7 @@
     masked_cot = cotangent * mask.astype(jnp.bfloat16)[None, :, :, None, None]
     full_width = chans * lax.axis_size("ch")
     carry = jnp.zeros((3, 9 * chans, full_width), jnp.float32)
-    piece = lax.all_gather(masked_cot, "ch", axis=0, tiled=True)
+    piece = gather_around(masked_cot, "ch", 0)
     start = jnp.int32(0)
     for time_tap in range(3):
         part = lax.dot_general(

time: 171 us -> 160 us (0.936)
  blocking collectives: 37 us -> 19.6 us
  starting transfers between devices: 14 us -> 18.7 us
  local copies, waits for them, and re-layouts: 9.05 us -> 12.7 us
  waiting for transfers between devices: 70.3 us -> 67.5 us
    all_gather x1 -> x0, blocking collectives: 17.3 us -> none  [body(): piece = lax.all_gather(masked_cot, 'ch', axis=0, tiled=True)]
    all_to_all x1, waiting for transfers between devices: 5.55 us -> 0.42 us  [body(): lax.all_to_all(normed, 'ch', split_axis=2, concat_axis=0, tiled=True)]
    ppermute x0 -> x3, waiting for transfers between devices: none -> 3.86 us  [gather_around(): block = lax.ppermute(block, axis, forward)]
    ppermute x0 -> x3, starting transfers between devices: none -> 3.81 us  [gather_around(): block = lax.ppermute(block, axis, forward)]
    dynamic_update_slice x0 -> x4, local copies, waits for them, and re-layouts: none -> 2.07 us  [gather_around(): out = lax.dynamic_update_slice_in_dim(out, block, owner * rows, axis=dim)]
    all_to_all x1, waiting for transfers between devices: 6.12 us -> 4.28 us  [body(): lax.all_to_all(projected, 'ch', split_axis=0, concat_axis=2, tiled=True)]
    unnamed x41 -> x45, local copies, waits for them, and re-layouts: 4.48 us -> 5.13 us
  transfers between devices with their start and end apart: 6 -> 9, of which waited for: 4 -> 6; matrix products, arithmetic and copies ran while one was open for 7% -> 13% of each run, Pallas kernels for 0% -> 0%
where the time goes in v1:
time: 160 us; the launch traced here: 159 us
  waiting for transfers between devices  67.5 us (42%)
  blocking collectives  19.6 us (12%)
  starting transfers between devices  18.7 us (12%)
  between operations  16.7 us (10%)
  local copies, waits for them, and re-layouts  12.7 us (8%)
  matrix products  12.2 us (8%)
  other arithmetic  11.4 us (7%)
    psum x1, waiting for transfers between devices, body(): lax.psum(grad_table.astype(jnp.bfloat16), ('ha', 'dp')).astype(jnp.float32)  53.8 us
    psum x2, blocking collectives, body(): first, second = lax.psum((first, second), 'ha')  10.8 us
    all_gather x1, blocking collectives, body(): piece = lax.all_gather(pairs, 'ha', axis=1, tiled=True)  8.81 us
    dot_general x3, matrix products, body(): lax.dot_general(part, stacks[time_tap], (((0,), (0,)), ((), ())), preferr...  5.73 us
    all_to_all x1, starting transfers between devices, body(): lax.all_to_all(normed, 'ch', split_axis=2, concat_axis=0, tiled=True)  5.41 us
    unnamed x45, local copies, waits for them, and re-layouts  5.13 us
    all_to_all x1, starting transfers between devices, body(): lax.all_to_all(projected, 'ch', split_axis=0, concat_axis=2, tiled=True)  4.52 us
    ppermute x1, waiting for transfers between devices, padded_2(): after = lax.ppermute(leading, axis, down)  4.32 us
  transfers between devices with their start and end apart: 9, of which 6 were waited for; matrix products, arithmetic and copies ran while one was open for 13% of the time, Pallas kernels for 0%

profile of v1, /device:TPU:0, one launch (start us, length us, event | category | flops | bytes accessed | tf_op | source)
XLA Modules:
  0.0 158.9 jit_solution(13526674115543186285)
XLA Ops:
  8.7 1.1 fusion.54
  10.4 5.9 %all-reduce.3 = (f32[8,1]{0,1:T(1,128)S(1)}, f32[8,1]{0,1:T(1,128)S(1)}) all-reduce(f32[8,1]{0,1:T(1,128)S(1)} %convolution_bitcast_fusion.3, f32[8,1]{0,1:T(1,128)S(1)} %convolution_bitcast_fusion.2), channel_id=1, replica_groups=mesh['ch'=4,'ha'=2,'dp'=4] {'ha'}, use_global_device_ids=true, to_apply=%region_2.0 | all-reduce | flops 16 | bytes 128 | tf_op jit(solution)/shard_map/psum | solution.py:109
  16.6 1.8 %fusion.75 = bf16[96,1,4,2,128]{4,0,3,1,2:T(8,128)(2,1)} fusion(f32[96]{0:T(128)} %param.16, f32[96]{0:T(128)} %param.15, f32[96]{0:T(128)S(1)} %mul.129, f32[96]{0:T(128)S(1)} %sub.75, bf16[96,1,4,2,128]{4,3,2,1,0:T(2,128)(2,1)} %param.13), kind=kLoop, calls=%fused_computation.81 | loop fusion | flops 589824 | bytes 394752 | tf_op jit(solution)/shard_map/convert_element_type | solution.py:110
  18.4 5.4 %all-to-all-start = ((bf16[96,1,4,2,128]{4,0,3,1,2:T(8,128)(2,1)}), bf16[96,1,4,2,128]{4,0,3,1,2:T(8,128)(2,1)S(1)}, u32[]{:S(2)}, u32[]{:S(2)}) async-start(bf16[96,1,4,2,128]{4,0,3,1,2:T(8,128)(2,1)} %fusion.75), calls=%async_computation | async-start | bytes 393216 | tf_op jit(solution)/shard_map/all_to_all | solution.py:113
  23.8 1.2 broadcast_multiply_fusion
  25.0 2.1 %collective-permute-start.2 = (bf16[96,1,4,2,128]{4,3,2,1,0:T(2,128)(2,1)S(1)}, bf16[96,1,4,2,128]{4,3,2,1,0:T(2,128)(2,1)}, u32[]{:S(2)}, u32[]{:S(2)}) collective-permute-start(bf16[96,1,4,2,128]{4,3,2,1,0:T(2,128)(2,1)S(1)} %broadcast_multiply_fusion), channel_id=1, source_target_pairs={{0,8},{8,16},{16,24},{24,0},{1,9},{9,17},{17,25},{25,1},{2,10},{10... | collective-permute-start | bytes 589832 | tf_op jit(solution)/shard_map/ppermute | solution.py:19
  27.1 2.8 %fusion.99 = (bf16[1,3,3,96,384]{4,3,2,1,0:T(8,128)(2,1)}, bf16[1,3,3,96,384]{4,3,2,1,0:T(8,128)(2,1)}, bf16[1,3,3,96,384]{4,3,2,1,0:T(8,128)(2,1)S(1)}) fusion(bf16[3,3,3,96,384]{4,3,2,1,0:T(8,128)(2,1)} %param.23), kind=kLoop, calls=%fused_computation.142 | loop fusion | bytes 3981312 | tf_op jit(solution)/shard_map/slice | solution.py:152
  29.9 0.2 fusion.117
  30.5 3.9 %collective-permute-done.2 = bf16[96,1,4,2,128]{4,3,2,1,0:T(2,128)(2,1)} collective-permute-done((bf16[96,1,4,2,128]{4,3,2,1,0:T(2,128)(2,1)S(1)}, bf16[96,1,4,2,128]{4,3,2,1,0:T(2,128)(2,1)}, u32[]{:S(2)}, u32[]{:S(2)}) %collective-permute-start.2) | collective-permute-done | bytes 196640 | tf_op jit(solution)/shard_map/ppermute | solution.py:19
  34.3 0.4 all-to-all-done
  34.9 0.4 fusion.37
  35.3 8.8 %all-gather = bf16[512,768]{1,0:T(8,128)(2,1)S(1)} all-gather(bf16[256,768]{1,0:T(8,128)(2,1)S(1)} %fusion.37), channel_id=2, replica_groups=mesh['ch'=4,'ha'=2,'dp'=4] {'ha'}, dimensions={0}, use_global_device_ids=true | all-gather | bytes 1179648 | tf_op jit(solution)/shard_map/all_gather | solution.py:132
  44.1 1.6 %fusion.101 = (f32[256]{0:T(256)S(1)}, f32[256,512]{1,0:T(8,128)S(1)}) fusion(bf16[1,512,768]{2,1,0:T(8,128)(2,1)S(1)} %bitcast.171, bf16[384,1152]{1,0:T(8,128)(2,1)} %param.17, f32[384]{0:T(512)S(1)} %slice-done, bf16[48,8,2,128]{3,2,1,0:T(2,128)(2,1)S(1)} %bitcast.179), kind=kOutput, calls=%fused_computation.144 | convolution fusion | flops 176619264 | bytes 1412096 | tf_op jit(solution)/shard_map/itc,isc->its/dot_general | solution.py:62
  45.7 0.2 fusion.48
  46.0 0.6 fusion.46
  46.6 0.9 copy.39
  47.4 4.5 %all-to-all-start.1 = ((bf16[384,1,1,2,128]{4,3,2,1,0:T(2,128)(2,1)}), bf16[384,1,1,2,128]{4,3,2,1,0:T(2,128)(2,1)S(1)}, u32[]{:S(2)}, u32[]{:S(2)}) async-start(bf16[384,1,1,2,128]{4,3,2,1,0:T(2,128)(2,1)} %copy.39), calls=%async_computation.1 | async-start | bytes 393216 | tf_op jit(solution)/shard_map/all_to_all | solution.py:139
  52.0 1.0 copy_dynamic-update-slice_fusion.2
  53.0 1.0 copy_dynamic-update-slice_fusion.1
  53.9 4.3 %all-to-all-done.1 = bf16[384,1,1,2,128]{4,3,2,1,0:T(2,128)(2,1)S(1)} async-done(((bf16[384,1,1,2,128]{4,3,2,1,0:T(2,128)(2,1)}), bf16[384,1,1,2,128]{4,3,2,1,0:T(2,128)(2,1)S(1)}, u32[]{:S(2)}, u32[]{:S(2)}) %all-to-all-start.1) | async-done | bytes 196640 | tf_op jit(solution)/shard_map/all_to_all | solution.py:139
  58.3 0.2 fusion.65
  59.1 1.7 %collective-permute-start.4 = (bf16[96,1,4,2,128]{4,3,2,1,0:T(2,128)(2,1)}, bf16[96,1,4,2,128]{4,3,2,1,0:T(2,128)(2,1)S(1)}, u32[]{:S(2)}, u32[]{:S(2)}) collective-permute-start(bf16[96,1,4,2,128]{4,3,2,1,0:T(2,128)(2,1)} %collective-permute-done.3), channel_id=1, source_target_pairs={{0,8},{8,16},{16,24},{24,0},{1,9},{9,17},{17,25},{25,1},{2,10},{10... | collective-permute-start | bytes 589832 | tf_op jit(solution)/shard_map/ppermute | solution.py:19
  60.8 4.9 %all-reduce.2 = (f32[8,1]{0,1:T(1,128)S(1)}, f32[8,1]{0,1:T(1,128)S(1)}) all-reduce(f32[8,1]{0,1:T(1,128)S(1)} %convolution_bitcast_fusion.1, f32[8,1]{0,1:T(1,128)S(1)} %convolution_bitcast_fusion), channel_id=1, replica_groups=mesh['ch'=4,'ha'=2,'dp'=4] {'ha'}, use_global_device_ids=true, to_apply=%region_10.11 | all-reduce | flops 16 | bytes 128 | tf_op jit(solution)/shard_map/psum | solution.py:142
  66.0 0.3 fusion.64
  66.4 3.4 %collective-permute-start = (bf16[96,1,4,1,128]{4,0,3,2,1:T(8,128)(2,1)S(1)}, bf16[96,1,4,1,128]{4,0,3,2,1:T(8,128)(2,1)S(1)}, u32[]{:S(2)}, u32[]{:S(2)}) collective-permute-start(bf16[96,1,4,1,128]{4,0,3,2,1:T(8,128)(2,1)S(1)} %get-tuple-element.47), channel_id=1, source_target_pairs={{0,4},{1,5},{2,6},{3,7},{8,12},{9,13},{10,14},{11,15},{16,20},{17,... | collective-permute-start | bytes 294920 | tf_op jit(solution)/shard_map/ppermute | solution.py:30
  69.8 1.3 collective-permute-start.1
  71.2 0.8 collective-permute-done
  72.0 4.3 %collective-permute-done.1 = bf16[96,1,4,1,128]{4,0,3,2,1:T(8,128)(2,1)S(1)} collective-permute-done((bf16[96,1,4,1,128]{4,0,3,2,1:T(8,128)(2,1)S(1)}, bf16[96,1,4,1,128]{4,0,3,2,1:T(8,128)(2,1)S(1)}, u32[]{:S(2)}, u32[]{:S(2)}) %collective-permute-start.1) | collective-permute-done | bytes 98336 | tf_op jit(solution)/shard_map/ppermute | solution.py:31
  76.3 0.4 fusion.41
  77.4 0.3 slice_dynamic-update-slice_fusion.10
  77.6 0.3 slice_dynamic-update-slice_fusion.9
  78.1 0.4 constant_dynamic-update-slice_fusion
  78.5 0.3 slice_dynamic-update-slice_fusion.7
  78.8 0.3 slice_dynamic-update-slice_fusion.6
  79.1 1.1 fusion.19
  80.9 0.6 copy-done.7
  81.4 1.2 fusion.25
  82.6 1.2 fusion.31
  83.8 1.3 copy-done.1
  85.1 0.2 reduce-scatter.2.cloned.1.call-start
  85.4 2.8 %fusion.11 = f32[4,2,128,384]{2,3,1,0:T(8,128)S(1)} fusion(bf16[864,384,1,1]{1,0,3,2:T(8,128)(2,1)} %bitcast.176, bf16[864,1,4,2,128]{4,0,3,2,1:T(8,128)(2,1)} %copy-done.9), kind=kOutput, calls=%fused_computation.14 | convolution fusion | flops 679477248 | bytes 4005888 | tf_op jit(solution)/shard_map/dot_general | solution.py:153
  88.2 1.0 fusion.15
  89.2 0.5 copy-done.3
  89.7 1.9 %fusion.34 = bf16[384,1,4,2,128]{4,0,3,2,1:T(8,128)(2,1)} fusion(bf16[864,384,1,1]{1,0,3,2:T(8,128)(2,1)S(1)} %bitcast.170, bf16[864,1,4,2,128]{4,0,3,2,1:T(8,128)(2,1)S(1)} %copy-done.3, f32[4,2,128,384]{2,3,1,0:T(8,128)S(1)} %fusion.15, f32[4,2,128,384]{2,3,1,0:T(8,128)S(1)} %fusion.11), kind=kOutput, calls=%fused_computation.26 | convolution fusion | flops 680656896 | bytes 6365184 | tf_op jit(solution)/shard_map/dot_general | solution.py:153
  91.7 53.8 %all-reduce.6.cloned.1.call-done = bf16[3,3,3,96,384]{4,3,2,1,0:T(8,128)(2,1)} async-done(((bf16[3,3,3,96,384]{4,3,2,1,0:T(8,128)(2,1)}), bf16[3,3,3,96,384]{4,3,2,1,0:T(8,128)(2,1)}) %all-reduce.6.cloned.1.call-update) | async-done | bytes 1990672 | tf_op jit(solution)/shard_map/psum | solution.py:180
  145.5 4.0 %convert_element_type.145 = f32[3,3,3,96,384]{4,3,2,1,0:T(8,128)} convert(bf16[3,3,3,96,384]{4,3,2,1,0:T(8,128)(2,1)} %all-reduce.6.cloned.1.call-done) | non-fusion elementwise | flops 995328 | bytes 5971968 | tf_op jit(solution)/shard_map/convert_element_type | solution.py:180
  149.5 1.1 fusion.68
  150.6 0.8 copy.49
  (83 shorter events, 3.7 us)
Async XLA Ops:
  8.0 38.0 %copy-start = (bf16[384,384]{1,0:T(8,128)(2,1)S(1)}, bf16[384,384]{1,0:T(8,128)(2,1)}, u32[]{:S(2)}) copy-start(bf16[384,384]{1,0:T(8,128)(2,1)} %param.19) | copy-start | bytes 884740
  18.4 16.3 %all-to-all-start = ((bf16[96,1,4,2,128]{4,0,3,1,2:T(8,128)(2,1)}), bf16[96,1,4,2,128]{4,0,3,1,2:T(8,128)(2,1)S(1)}, u32[]{:S(2)}, u32[]{:S(2)}) async-start(bf16[96,1,4,2,128]{4,0,3,1,2:T(8,128)(2,1)} %fusion.75), calls=%async_computation | async-start | bytes 393216 | tf_op jit(solution)/shard_map/all_to_all | solution.py:113
  25.0 4.9 %copy-start.5 = (bf16[96,1,4,2,128]{4,3,2,1,0:T(2,128)(2,1)S(1)}, bf16[96,1,4,2,128]{4,3,2,1,0:T(2,128)(2,1)}, u32[]{:S(2)}) copy-start(bf16[96,1,4,2,128]{4,3,2,1,0:T(2,128)(2,1)} %param.25) | copy-start | bytes 589828
  25.0 5.2 %copy-start.12 = (f32[1152]{0:T(1024)S(1)}, f32[1152]{0:T(1024)}, u32[]{:S(2)}) copy-start(f32[1152]{0:T(1024)} %param.18) | copy-start | bytes 13828
  25.0 9.3 %collective-permute-start.2 = (bf16[96,1,4,2,128]{4,3,2,1,0:T(2,128)(2,1)S(1)}, bf16[96,1,4,2,128]{4,3,2,1,0:T(2,128)(2,1)}, u32[]{:S(2)}, u32[]{:S(2)}) collective-permute-start(bf16[96,1,4,2,128]{4,3,2,1,0:T(2,128)(2,1)S(1)} %broadcast_multiply_fusion), channel_id=1, source_target_pairs={{0,8},{8,16},{16,24},{24,0},{1,9},{9,17},{17,25},{25,1},{2,10},{10... | collective-permute-start | bytes 589832 | tf_op jit(solution)/shard_map/ppermute | solution.py:19
  29.9 5.0 %copy-start.16 = (bf16[384,1152]{1,0:T(8,128)(2,1)S(1)}, bf16[384,1152]{1,0:T(8,128)(2,1)}, u32[]{:S(2)}) copy-start(bf16[384,1152]{1,0:T(8,128)(2,1)} %param.17) | copy-start | bytes 2654212
  30.4 13.7 %slice-start = ((f32[1152]{0:T(1024)}), f32[384]{0:T(512)S(1)}, s32[]{:S(2)}) async-start(f32[1152]{0:T(1024)} %param.18), calls=%async_computation.5 | async-start | bytes 4096 | tf_op jit(solution)/shard_map/slice | solution.py:121
  34.3 18.6 %collective-permute-start.3 = (bf16[96,1,4,2,128]{4,3,2,1,0:T(2,128)(2,1)}, bf16[96,1,4,2,128]{4,3,2,1,0:T(2,128)(2,1)}, u32[]{:S(2)}, u32[]{:S(2)}) collective-permute-start(bf16[96,1,4,2,128]{4,3,2,1,0:T(2,128)(2,1)} %collective-permute-done.2), channel_id=1, source_target_pairs={{0,8},{8,16},{16,24},{24,0},{1,9},{9,17},{17,25},{25,1},{2,10},{10... | collective-permute-start | bytes 589832 | tf_op jit(solution)/shard_map/ppermute | solution.py:19
  35.3 10.7 %copy-start.17 = (f32[384]{0:T(512)S(1)}, f32[384]{0:T(512)}, u32[]{:S(2)}) copy-start(f32[384]{0:T(512)} %param.20) | copy-start | bytes 4612
  46.0 12.3 %copy-start.4 = (bf16[96,1,4,2,128]{4,3,2,1,0:T(2,128)(2,1)S(1)}, bf16[96,1,4,2,128]{4,3,2,1,0:T(2,128)(2,1)}, u32[]{:S(2)}) copy-start(bf16[96,1,4,2,128]{4,3,2,1,0:T(2,128)(2,1)} %param.13) | copy-start | bytes 589828
  46.6 19.5 %copy-start.13 = (f32[96]{0:T(128)S(1)}, f32[96]{0:T(128)}, u32[]{:S(2)}) copy-start(f32[96]{0:T(128)} %param.22) | copy-start | bytes 1156
  46.6 19.5 %copy-start.14 = (f32[96]{0:T(128)S(1)}, f32[96]{0:T(128)}, u32[]{:S(2)}) copy-start(f32[96]{0:T(128)} %param.21) | copy-start | bytes 1156
  47.4 10.8 %all-to-all-start.1 = ((bf16[384,1,1,2,128]{4,3,2,1,0:T(2,128)(2,1)}), bf16[384,1,1,2,128]{4,3,2,1,0:T(2,128)(2,1)S(1)}, u32[]{:S(2)}, u32[]{:S(2)}) async-start(bf16[384,1,1,2,128]{4,3,2,1,0:T(2,128)(2,1)} %copy.39), calls=%async_computation.1 | async-start | bytes 393216 | tf_op jit(solution)/shard_map/all_to_all | solution.py:139
  52.0 93.6 %all-reduce.6.cloned.1.call-start = ((), (), s32[]{:S(2)}) async-start(), calls=%async_computation.4 | async-start | bytes 3981312 | tf_op jit(solution)/shard_map/psum | solution.py:180
  59.1 12.1 %collective-permute-start.4 = (bf16[96,1,4,2,128]{4,3,2,1,0:T(2,128)(2,1)}, bf16[96,1,4,2,128]{4,3,2,1,0:T(2,128)(2,1)S(1)}, u32[]{:S(2)}, u32[]{:S(2)}) collective-permute-start(bf16[96,1,4,2,128]{4,3,2,1,0:T(2,128)(2,1)} %collective-permute-done.3), channel_id=1, source_target_pairs={{0,8},{8,16},{16,24},{24,0},{1,9},{9,17},{17,25},{25,1},{2,10},{10... | collective-permute-start | bytes 589832 | tf_op jit(solution)/shard_map/ppermute | solution.py:19
  66.4 5.6 %collective-permute-start = (bf16[96,1,4,1,128]{4,0,3,2,1:T(8,128)(2,1)S(1)}, bf16[96,1,4,1,128]{4,0,3,2,1:T(8,128)(2,1)S(1)}, u32[]{:S(2)}, u32[]{:S(2)}) collective-permute-start(bf16[96,1,4,1,128]{4,0,3,2,1:T(8,128)(2,1)S(1)} %get-tuple-element.47), channel_id=1, source_target_pairs={{0,4},{1,5},{2,6},{3,7},{8,12},{9,13},{10,14},{11,15},{16,20},{17,... | collective-permute-start | bytes 294920 | tf_op jit(solution)/shard_map/ppermute | solution.py:30
  69.8 6.5 %collective-permute-start.1 = (bf16[96,1,4,1,128]{4,0,3,2,1:T(8,128)(2,1)S(1)}, bf16[96,1,4,1,128]{4,0,3,2,1:T(8,128)(2,1)S(1)}, u32[]{:S(2)}, u32[]{:S(2)}) collective-permute-start(bf16[96,1,4,1,128]{4,0,3,2,1:T(8,128)(2,1)S(1)} %get-tuple-element.48), channel_id=1, source_target_pairs={{4,0},{5,1},{6,2},{7,3},{12,8},{13,9},{14,10},{15,11},{20,16},{21,... | collective-permute-start | bytes 294920 | tf_op jit(solution)/shard_map/ppermute | solution.py:31
  71.2 7.9 %copy-start.6 = (bf16[384,4,2,128]{3,0,2,1:T(8,128)(2,1)}, bf16[384,4,2,128]{3,0,2,1:T(8,128)(2,1)S(1)}, u32[]{:S(2)}) copy-start(bf16[384,4,2,128]{3,0,2,1:T(8,128)(2,1)S(1)} %copy_dynamic-update-slice_fusion) | copy-start | bytes 2359300
  79.1 1.2 copy-start.10
  79.1 1.8 %copy-start.9 = (bf16[864,1,4,2,128]{4,0,3,2,1:T(8,128)(2,1)}, bf16[864,1,4,2,128]{4,0,3,2,1:T(8,128)(2,1)S(1)}, u32[]{:S(2)}) copy-start(bf16[864,1,4,2,128]{4,0,3,2,1:T(8,128)(2,1)S(1)} %get-tuple-element.24) | copy-start | bytes 5308420
  80.3 1.1 copy-start.7
  80.7 2.0 %copy-start.2 = (bf16[864,1,4,2,128]{4,0,3,2,1:T(8,128)(2,1)}, bf16[864,1,4,2,128]{4,0,3,2,1:T(8,128)(2,1)S(1)}, u32[]{:S(2)}) copy-start(bf16[864,1,4,2,128]{4,0,3,2,1:T(8,128)(2,1)S(1)} %slice_dynamic-update-slice_fusion) | copy-start | bytes 5308420
  83.8 1.3 copy-start.1
  85.1 64.4 %reduce-scatter.2.cloned.1.call-start = ((), (), s32[]{:S(2)}) async-start(), calls=%async_computation.3 | async-start | bytes 983040 | tf_op jit(solution)/shard_map/reduce_scatter | solution.py:156
  85.3 2.8 %copy-start.8 = (bf16[1,3,3,96,384]{4,3,2,1,0:T(8,128)(2,1)S(1)}, bf16[1,3,3,96,384]{4,3,2,1,0:T(8,128)(2,1)}, u32[]{:S(2)}) copy-start(bf16[1,3,3,96,384]{4,3,2,1,0:T(8,128)(2,1)} %get-tuple-element.22) | copy-start | bytes 1990660
  85.3 2.8 %copy-start.11 = (bf16[864,1,4,2,128]{4,0,3,2,1:T(8,128)(2,1)S(1)}, bf16[864,1,4,2,128]{4,0,3,2,1:T(8,128)(2,1)}, u32[]{:S(2)}) copy-start(bf16[864,1,4,2,128]{4,0,3,2,1:T(8,128)(2,1)} %copy-done.10) | copy-start | bytes 5308420
  88.2 1.6 copy-start.3
  91.7 57.8 %copy-start.15 = (f32[96]{0:T(128)S(1)}, f32[96]{0:T(128)}, u32[]{:S(2)}) copy-start(f32[96]{0:T(128)} %param.24) | copy-start | bytes 1156
Sparse Core Ops, SparseCore 0:
  85.2 60.2 all-reduce.5
Sparse Core Ops, SparseCore 1:
  91.8 22.0 reduce-scatter.1
